TPU v7x, 32 devices: a whole 2x2x4 slice. The times are simulated.
32 devices in a mesh: row: 2 (over x), col: 4 (over y, core), grid: 4 (over z).
Axes of the slice: x: 2, y: 2, z: 4, core: 2. Of those that a mesh axis runs over, the one named last changes fastest.
Arguments:
- snapshots: bfloat16 [16384, 1024], P(('row', 'col', 'grid')), may hold values from -6 to 6
- jitter_code: int32 [16384], replicated, may hold values from 0 to 63
- slab_start: int32 [4], P('grid'), may hold values from 0 to 127
- gamma: float32 [2048], P('grid'), may hold values from 0.1 to 10
- noise_var: float32 [1], replicated, may hold values from 0.3 to 1.5
Outputs:
- steered: float32 [16384, 2048], P(('row', 'col'), 'grid')
- gamma_new: float32 [2048], P('grid')
All inputs are finite; a program needn't handle non-finite values.
Results may differ from a plain program's by a relative error of at most 0.0003.
Values may be sent and summed in bfloat16 or wider, within the bound.
A program may use at most 64 MiB of HBM per device.

v0:
```python
import jax
import jax.numpy as jnp
from jax import lax
from jax.sharding import PartitionSpec as P

SNAP = 1024
GRID = 65536


def steer(sensor, codes, points):
    pos = (64 * sensor + codes + 32)[:, None]
    low = (points % 256)[None, :]
    high = (points // 256)[None, :]
    modulus = 64 * GRID
    first = pos * low % modulus
    second = pos * high % (modulus // 256) * 256
    wound = (first + second) % modulus
    turns = wound.astype(jnp.float32) / modulus - (pos % 128).astype(jnp.float32) / 128.0
    return jnp.cos(2.0 * jnp.pi * turns)


def on_device(snapshots, jitter_code, slab_start, gamma, noise_var):
    n_col = lax.axis_size("col")
    n_grid = lax.axis_size("grid")
    own_count = snapshots.shape[0]
    group_rows = own_count * n_grid
    block_rows = group_rows * n_col
    row_id = lax.axis_index("row")
    col_id = lax.axis_index("col")
    slab_len = gamma.shape[0]
    stride = GRID // slab_len
    points = slab_start[0] + stride * jnp.arange(slab_len, dtype=jnp.int32)
    own_sensors = (
        row_id * block_rows + col_id * group_rows + jnp.arange(group_rows, dtype=jnp.int32)
    )
    own_snaps = lax.all_gather(snapshots, "grid", axis=0, tiled=True).astype(jnp.float32)
    own_steer = steer(own_sensors, jnp.take(jitter_code, own_sensors), points)
    partial_value = jnp.dot(own_snaps.T, own_steer, precision=lax.Precision.HIGHEST)
    projected, norms = lax.psum(
        (partial_value, jnp.sum(own_steer * own_steer, axis=0)), ("row", "col")
    )
    steered = jnp.dot(own_snaps, projected, precision=lax.Precision.HIGHEST) / SNAP
    forms = jnp.sum(projected * projected, axis=0) / SNAP
    gamma_new = gamma * forms / (norms * (gamma + noise_var[0]))
    return (steered, gamma_new)


def solution(mesh):
    in_specs = (P(("row", "col", "grid"), None), P(), P("grid"), P("grid"), P())
    out_specs = (P(("row", "col"), "grid"), P("grid"))
    return jax.shard_map(
        on_device, mesh=mesh, in_specs=in_specs, out_specs=out_specs, check_vma=False
    )
```

profile of v0, /device:TPU:0, one launch (start us, length us, event | category | flops | bytes accessed | tf_op | source)
XLA Modules:
  0.0 206.2 jit_solution(13674816523971793353)
XLA Ops:
  7.2 0.0 copy-start
  7.2 0.0 all-gather.2.cloned.1.call-start
  7.2 0.7 all-gather.2.cloned.1.call-update
  7.9 0.0 all-reduce.2.cloned.1.call-start
  9.3 0.0 copy-done
  9.3 11.8 %gather_fusion = s32[2048]{0:T(1024)S(1)} fusion(s32[16384]{0:T(1024)S(1)} %copy-done, s32[2048]{0:T(1024)S(1)} %broadcast_clamp_fusion), kind=kCustom, calls=%fused_computation | custom fusion | bytes 24576 | tf_op jit(solution)/shard_map/jit(_take)/gather | solution.py:37
  21.1 71.9 %all-gather.2.cloned.1.call-done = bf16[2048,1024]{1,0:T(8,128)(2,1)} async-done(((bf16[512,1024]{1,0:T(8,128)(2,1)}), bf16[2048,1024]{1,0:T(8,128)(2,1)}) %all-gather.2.cloned.1.call-update) | async-done | bytes 4194320 | tf_op jit(solution)/shard_map/all_gather | solution.py:36
  93.1 28.9 %fusion.12 = f32[1024,512]{0,1:T(8,128)} fusion(bf16[2048,1024]{1,0:T(8,128)(2,1)} %all-gather.2.cloned.1.call-done, f32[2048]{0:T(1024)S(1)} %get-tuple-element.8, s32[512]{0:T(512)S(1)} %get-tuple-element.10, s32[512]{0:T(512)S(1)} %get-tuple-element.11, s32[2048]{0:T(1024)S(1)} %get-tuple-element.9), kind=kOutput, calls=%fused_computation.28 | convolution fusion | flops 12927893504 | bytes 6311936 | tf_op jit(solution)/shard_map/dot_general | solution.py:38
  122.0 0.0 all-reduce.2.cloned.1.call-update
  122.0 20.6 %multiply_reduce_fusion = f32[512]{0:T(512)S(1)} fusion(f32[2048]{0:T(1024)S(1)} %get-tuple-element.8, s32[512]{0:T(512)S(1)} %get-tuple-element.10, s32[512]{0:T(512)S(1)} %get-tuple-element.11, s32[2048]{0:T(1024)S(1)} %get-tuple-element.9), kind=kLoop, calls=%fused_computation.24 | loop fusion | flops 45088256 | bytes 22528 | tf_op jit(solution)/shard_map/reduce_sum | solution.py:40
  142.6 13.7 %psum.15 = f32[512]{0:T(512)S(1)} all-reduce(f32[512]{0:T(512)S(1)} %multiply_reduce_fusion), channel_id=1, replica_groups=mesh['row'=2,'col'=4,'grid'=4] {'row','col'}, use_global_device_ids=true, to_apply=%region_3.4 | all-reduce | flops 512 | bytes 4096 | tf_op jit(solution)/shard_map/psum | solution.py:39
  156.4 26.2 %all-reduce.2.cloned.1.call-done = f32[1024,512]{0,1:T(8,128)} async-done(((f32[1024,512]{0,1:T(8,128)}), f32[1024,512]{0,1:T(8,128)}) %all-reduce.2.cloned.1.call-update) | async-done | bytes 2097168 | tf_op jit(solution)/shard_map/psum | solution.py:39
  182.6 10.5 %multiply_bitcast_fusion = f32[2048,512]{0,1:T(8,128)} fusion(f32[1024,512]{0,1:T(8,128)} %all-reduce.2.cloned.1.call-done, bf16[2048,1024]{1,0:T(8,128)(2,1)} %all-gather.2.cloned.1.call-done), kind=kOutput, calls=%fused_computation.25 | convolution fusion | flops 12885950464 | bytes 10485760 | tf_op jit(solution)/shard_map/dot_general | solution.py:42
  193.0 0.0 copy-start.1
  193.0 0.0 copy-start.2
  193.0 5.5 %copy.9 = f32[2048,512]{1,0:T(8,128)} copy(f32[2048,512]{0,1:T(8,128)} %multiply_bitcast_fusion) | data formatting | bytes 8388608
  198.5 0.0 copy-done.1
  198.5 0.2 multiply_reduce_fusion.1
  198.7 0.0 copy-done.2
  198.7 0.6 multiply_divide_fusion
  (4 shorter events, 0.1 us)
Async XLA Ops:
  7.2 2.1 %copy-start = (s32[16384]{0:T(1024)S(1)}, s32[16384]{0:T(1024)}, u32[]{:S(2)}) copy-start(s32[16384]{0:T(1024)} %param.6) | copy-start | bytes 196612
  7.2 85.9 %all-gather.2.cloned.1.call-start = ((), (), s32[]{:S(2)}) async-start(), calls=%async_computation | async-start | bytes 5242880 | tf_op jit(solution)/shard_map/all_gather | solution.py:36
  7.9 174.6 %all-reduce.2.cloned.1.call-start = ((), (), s32[]{:S(2)}) async-start(), calls=%async_computation.1 | async-start | bytes 4194304 | tf_op jit(solution)/shard_map/psum | solution.py:39
  193.0 5.5 %copy-start.1 = (f32[1024,512]{0,1:T(8,128)S(1)}, f32[1024,512]{0,1:T(8,128)}, u32[]{:S(2)}) copy-start(f32[1024,512]{0,1:T(8,128)} %all-reduce.2.cloned.1.call-done) | copy-start | bytes 6291460
  193.0 5.7 %copy-start.2 = (f32[512]{0:T(512)S(1)}, f32[512]{0:T(512)}, u32[]{:S(2)}) copy-start(f32[512]{0:T(512)} %param.8) | copy-start | bytes 6148
Sparse Core Ops, SparseCore 0:
  9.6 83.4 all-gather.1
  122.1 60.3 all-reduce.1
where the time goes:
time: 206 us
  waiting for transfers between devices  98.8 us (48%)
  matrix products  39.4 us (19%)
  other arithmetic  21.5 us (10%)
  local copies, waits for them, and re-layouts  17.3 us (8%)
  between operations  15.4 us (7%)
  blocking collectives  13.7 us (7%)
    all_gather x1, waiting for transfers between devices, on_device(): lax.all_gather(snapshots, 'grid', axis=0, tiled=True).astype(jnp.float32)  71.9 us
    dot_general x1, matrix products, on_device(): jnp.dot(own_snaps.T, own_steer, precision=lax.Precision.HIGHEST)  28.9 us
    psum x1, waiting for transfers between devices, on_device(): lax.psum((partial_value, jnp.sum(own_steer * own_steer, axis=0)), ('row',...  26.2 us
    reduce_sum x1, other arithmetic, on_device(): jnp.sum(own_steer * own_steer, axis=0)  20.6 us
    psum x1, blocking collectives, on_device(): lax.psum((partial_value, jnp.sum(own_steer * own_steer, axis=0)), ('row',...  13.7 us
    gather x1, local copies, waits for them, and re-layouts, on_device(): own_steer = steer(own_sensors, jnp.take(jitter_code, own_sensors), points)  11.8 us
    dot_general x1, matrix products, on_device(): jnp.dot(own_snaps, projected, precision=lax.Precision.HIGHEST) / SNAP  10.5 us
    unnamed x7, local copies, waits for them, and re-layouts  5.51 us
  transfers between devices with their start and end apart: 2, of which 2 were waited for; matrix products, arithmetic and copies ran while one was open for 16% of the time, Pallas kernels for 0%

commit v1 on v0

v1 whole, which is shorter than its diff:
```python
import jax
import jax.numpy as jnp
from jax import lax
from jax.sharding import PartitionSpec as P

SNAP = 1024
GRID = 65536


def sine(turns):
    z = turns * turns
    p = jnp.float32(39.53581371)
    p = p * z + jnp.float32(-76.54965682)
    p = p * z + jnp.float32(81.60099819)
    p = p * z + jnp.float32(-41.34165493)
    p = p * z + jnp.float32(6.28318516)
    return p * turns


def steer(sensor, codes, points):
    pos = 64 * sensor + codes + 32
    phase = (pos[:, None] * points[None, :] - ((pos & 127) << 15)[:, None]) << 10
    turns = phase.astype(jnp.float32) * jnp.float32(2.0**-32)
    return sine(0.25 - jnp.abs(turns))


def split(x):
    hi = lax.reduce_precision(x, 8, 7)
    lo = x - hi
    return hi.astype(jnp.bfloat16), lo.astype(jnp.bfloat16)


def on_device(snapshots, jitter_code, slab_start, gamma, noise_var):
    n_col = lax.axis_size("col")
    n_grid = lax.axis_size("grid")
    own_count = snapshots.shape[0]
    group_rows = own_count * n_grid
    block_rows = group_rows * n_col
    row_id = lax.axis_index("row")
    col_id = lax.axis_index("col")
    slab_len = gamma.shape[0]
    stride = GRID // slab_len
    points = slab_start[0] + stride * jnp.arange(slab_len, dtype=jnp.int32)
    base = row_id * block_rows + col_id * group_rows
    own_sensors = base + jnp.arange(group_rows, dtype=jnp.int32)
    codes = lax.dynamic_slice(jitter_code, (base,), (group_rows,))
    own_snaps = lax.all_gather(snapshots, "grid", axis=0, tiled=True)
    own_steer = steer(own_sensors, codes, points)
    hi, lo = split(own_steer)
    dn = (((0,), (0,)), ((), ()))
    f32 = jnp.float32
    partial_value = lax.dot_general(own_snaps, hi, dn, preferred_element_type=f32)
    partial_value += lax.dot_general(own_snaps, lo, dn, preferred_element_type=f32)
    projected, norms = lax.psum(
        (partial_value, jnp.sum(own_steer * own_steer, axis=0)), ("row", "col")
    )
    hi, lo = split(projected)
    steered = jnp.dot(own_snaps, hi, preferred_element_type=f32)
    steered += jnp.dot(own_snaps, lo, preferred_element_type=f32)
    steered = steered / SNAP
    forms = jnp.sum(projected * projected, axis=0) / SNAP
    gamma_new = gamma * forms / (norms * (gamma + noise_var[0]))
    return (steered, gamma_new)


def solution(mesh):
    in_specs = (P(("row", "col", "grid"), None), P(), P("grid"), P("grid"), P())
    out_specs = (P(("row", "col"), "grid"), P("grid"))
    return jax.shard_map(
        on_device, mesh=mesh, in_specs=in_specs, out_specs=out_specs, check_vma=False
    )
```

time: 206 us -> 188 us (0.913)
  waiting for transfers between devices: 98.8 us -> 128 us
  matrix products: 39.4 us -> 21.4 us
  other arithmetic: 21.5 us -> 4.48 us
  local copies, waits for them, and re-layouts: 17.3 us -> 5.36 us
    dot_general x2 -> x4, matrix products: 39.4 us -> 21.4 us  [the longest x1 6.47 us: on_device(): lax.dot_general(own_snaps, lo, dn, preferred_element_type=f32)]
    reduce_sum x1, other arithmetic: 20.6 us -> 2.96 us  [on_device(): jnp.sum(own_steer * own_steer, axis=0)]
    psum x1, waiting for transfers between devices: 26.2 us -> 43.2 us  [on_device(): lax.psum((partial_value, jnp.sum(own_steer * own_steer, axis=0)), ('row',...]
    all_gather x1, waiting for transfers between devices: 71.9 us -> 83.7 us  [on_device(): own_snaps = lax.all_gather(snapshots, 'grid', axis=0, tiled=True)]
    gather x1 -> x0, local copies, waits for them, and re-layouts: 11.8 us -> none  [on_device(): own_steer = steer(own_sensors, jnp.take(jitter_code, own_sensors), points)]
    unnamed x7 -> x9, local copies, waits for them, and re-layouts: 5.51 us -> 5.36 us
  transfers between devices with their start and end apart: 2 -> 2, of which waited for: 2 -> 2; matrix products, arithmetic and copies ran while one was open for 16% -> 2% of each run, Pallas kernels for 0% -> 0%
where the time goes in v1:
time: 188 us
  waiting for transfers between devices  128 us (68%)
  matrix products  21.4 us (11%)
  between operations  15.4 us (8%)
  blocking collectives  13.8 us (7%)
  local copies, waits for them, and re-layouts  5.36 us (3%)
  other arithmetic  4.48 us (2%)
    all_gather x1, waiting for transfers between devices, on_device(): own_snaps = lax.all_gather(snapshots, 'grid', axis=0, tiled=True)  83.7 us
    psum x1, waiting for transfers between devices, on_device(): lax.psum((partial_value, jnp.sum(own_steer * own_steer, axis=0)), ('row',...  43.2 us
    psum x1, blocking collectives, on_device(): lax.psum((partial_value, jnp.sum(own_steer * own_steer, axis=0)), ('row',...  13.8 us
    dot_general x1, matrix products, on_device(): lax.dot_general(own_snaps, lo, dn, preferred_element_type=f32)  6.47 us
    unnamed x9, local copies, waits for them, and re-layouts  5.36 us
    dot_general x1, matrix products, on_device(): steered = jnp.dot(own_snaps, hi, preferred_element_type=f32)  5.33 us
    dot_general x1, matrix products, on_device(): lax.dot_general(own_snaps, hi, dn, preferred_element_type=f32)  5.21 us
    dot_general x1, matrix products, on_device(): steered += jnp.dot(own_snaps, lo, preferred_element_type=f32)  4.34 us
  transfers between devices with their start and end apart: 2, of which 2 were waited for; matrix products, arithmetic and copies ran while one was open for 2% of the time, Pallas kernels for 0%

profile of v1, /device:TPU:0, one launch (start us, length us, event | category | flops | bytes accessed | tf_op | source)
XLA Modules:
  0.0 188.0 jit_solution(4822104468102924864)
XLA Ops:
  7.2 0.0 all-gather.2.cloned.1.call-start
  7.2 0.7 all-gather.2.cloned.1.call-update
  7.9 0.0 all-reduce.2.cloned.1.call-start
  8.6 0.7 and_shift-left_fusion
  9.3 83.7 %all-gather.2.cloned.1.call-done = bf16[2048,1024]{1,0:T(8,128)(2,1)} async-done(((bf16[512,1024]{1,0:T(8,128)(2,1)}), bf16[2048,1024]{1,0:T(8,128)(2,1)}) %all-gather.2.cloned.1.call-update) | async-done | bytes 4194320 | tf_op jit(solution)/shard_map/all_gather | solution.py:47
  93.0 0.0 copy-start.2
  93.0 6.5 %fusion.4 = f32[512,1024]{1,0:T(8,128)S(1)} fusion(bf16[2048,1024]{1,0:T(8,128)(2,1)} %all-gather.2.cloned.1.call-done, s32[2048]{0:T(1024)S(1)} %get-tuple-element.6, s32[512]{0:T(512)S(1)} %multiply_add_fusion, s32[2048]{0:T(1024)S(1)} %get-tuple-element.7), kind=kOutput, calls=%fused_computation.13 | convolution fusion | flops 2168455168 | bytes 6309888 | tf_op jit(solution)/shard_map/dot_general | solution.py:53
  99.5 0.0 copy-done.2
  99.5 5.2 %add_bitcast_fusion = f32[1024,512]{0,1:T(8,128)} fusion(f32[512,1024]{1,0:T(8,128)S(1)} %fusion.4, bf16[2048,1024]{1,0:T(8,128)(2,1)S(1)} %copy-done.2, s32[2048]{0:T(1024)S(1)} %get-tuple-element.6, s32[512]{0:T(512)S(1)} %multiply_add_fusion, s32[2048]{0:T(1024)S(1)} %get-tuple-element.7), kind=kOutput, calls=%fused_computation.16 | convolution fusion | flops 2167930880 | bytes 8407040 | tf_op jit(solution)/shard_map/dot_general | solution.py:52
  104.7 0.0 all-reduce.2.cloned.1.call-update
  105.4 3.0 %multiply_reduce_fusion = f32[512]{0:T(512)S(1)} fusion(s32[2048]{0:T(1024)S(1)} %get-tuple-element.6, s32[512]{0:T(512)S(1)} %multiply_add_fusion, s32[2048]{0:T(1024)S(1)} %get-tuple-element.7), kind=kLoop, calls=%fused_computation.3 | loop fusion | flops 19922432 | bytes 20480 | tf_op jit(solution)/shard_map/reduce_sum | solution.py:55
  108.4 13.8 %psum.15 = f32[512]{0:T(512)S(1)} all-reduce(f32[512]{0:T(512)S(1)} %multiply_reduce_fusion), channel_id=1, replica_groups=mesh['row'=2,'col'=4,'grid'=4] {'row','col'}, use_global_device_ids=true, to_apply=%region_3.0 | all-reduce | flops 512 | bytes 4096 | tf_op jit(solution)/shard_map/psum | solution.py:54
  122.1 43.2 %all-reduce.2.cloned.1.call-done = f32[1024,512]{0,1:T(8,128)} async-done(((f32[1024,512]{0,1:T(8,128)}), f32[1024,512]{0,1:T(8,128)}) %all-reduce.2.cloned.1.call-update) | async-done | bytes 2097168 | tf_op jit(solution)/shard_map/psum | solution.py:54
  165.3 0.0 copy-start
  165.3 0.0 copy-start.3
  165.3 5.3 %fusion.8 = f32[512,2048]{1,0:T(8,128)S(1)} fusion(bf16[2048,1024]{1,0:T(8,128)(2,1)} %all-gather.2.cloned.1.call-done, f32[1024,512]{0,1:T(8,128)} %all-reduce.2.cloned.1.call-done), kind=kOutput, calls=%fused_computation.17 | convolution fusion | flops 2148532224 | bytes 10485760 | tf_op jit(solution)/shard_map/dot_general | solution.py:58
  170.7 0.0 copy-done
  170.7 0.0 copy-done.3
  170.7 4.3 %multiply_bitcast_fusion = f32[2048,512]{0,1:T(8,128)} fusion(f32[512,2048]{1,0:T(8,128)S(1)} %fusion.8, bf16[2048,1024]{1,0:T(8,128)(2,1)S(1)} %copy-done.3, f32[1024,512]{0,1:T(8,128)S(1)} %copy-done), kind=kOutput, calls=%fused_computation.4 | convolution fusion | flops 2151153664 | bytes 14680064 | tf_op jit(solution)/shard_map/dot_general | solution.py:59
  175.0 0.0 copy-start.1
  175.0 5.3 %copy.8 = f32[2048,512]{1,0:T(8,128)} copy(f32[2048,512]{0,1:T(8,128)} %multiply_bitcast_fusion) | data formatting | bytes 8388608
  180.4 0.2 multiply_reduce_fusion.1
  180.6 0.0 copy-done.1
  180.6 0.6 multiply_divide_fusion
  (1 shorter events, 0.0 us)
Async XLA Ops:
  7.2 85.9 %all-gather.2.cloned.1.call-start = ((), (), s32[]{:S(2)}) async-start(), calls=%async_computation | async-start | bytes 5242880 | tf_op jit(solution)/shard_map/all_gather | solution.py:47
  7.9 157.4 %all-reduce.2.cloned.1.call-start = ((), (), s32[]{:S(2)}) async-start(), calls=%async_computation.1 | async-start | bytes 4194304 | tf_op jit(solution)/shard_map/psum | solution.py:54
  93.0 6.5 %copy-start.2 = (bf16[2048,1024]{1,0:T(8,128)(2,1)S(1)}, bf16[2048,1024]{1,0:T(8,128)(2,1)}, u32[]{:S(2)}) copy-start(bf16[2048,1024]{1,0:T(8,128)(2,1)} %all-gather.2.cloned.1.call-done) | copy-start | bytes 12582916
  165.3 5.3 %copy-start = (f32[1024,512]{0,1:T(8,128)S(1)}, f32[1024,512]{0,1:T(8,128)}, u32[]{:S(2)}) copy-start(f32[1024,512]{0,1:T(8,128)} %all-reduce.2.cloned.1.call-done) | copy-start | bytes 6291460
  165.3 5.4 %copy-start.3 = (bf16[2048,1024]{1,0:T(8,128)(2,1)S(1)}, bf16[2048,1024]{1,0:T(8,128)(2,1)}, u32[]{:S(2)}) copy-start(bf16[2048,1024]{1,0:T(8,128)(2,1)} %all-gather.2.cloned.1.call-done) | copy-start | bytes 12582916
  175.0 5.6 %copy-start.1 = (f32[512]{0:T(512)S(1)}, f32[512]{0:T(512)}, u32[]{:S(2)}) copy-start(f32[512]{0:T(512)} %param.8) | copy-start | bytes 6148
Sparse Core Ops, SparseCore 0:
  9.5 83.4 all-gather.1
  104.9 60.3 all-reduce.1

commit v2 on v0

v2 whole, which is shorter than its diff:
```python
import functools

import jax
import jax.numpy as jnp
from jax import lax
from jax.experimental import pallas as pl
from jax.experimental.pallas import tpu as pltpu
from jax.sharding import PartitionSpec as P

GRID = 65536
WIDTH = 256
F32 = jnp.float32
BF16 = jnp.bfloat16
MESH = pl.DeviceIdType.MESH


def sine(turns):
    z = turns * turns
    p = F32(39.53581371)
    p = p * z + F32(-76.54965682)
    p = p * z + F32(81.60099819)
    p = p * z + F32(-41.34165493)
    p = p * z + F32(6.28318516)
    return p * turns


def split(x):
    hi = x.astype(BF16)
    return hi, (x - hi.astype(F32)).astype(BF16)


def kernel(
    sizes, start_ref, pos_ref, snaps_ref, out_ref, forms_ref, norms_ref,
    held, steer_hi, steer_lo, part, part_norm, full, proj_hi, proj_lo, *rest,
):
    n_row, n_col, n_grid, stride = sizes
    dims = [d for d in ((2, "core"), (n_col // 2, "y"), (n_row, "row")) if d[0] > 1]
    landed, sums = rest[: len(dims)], rest[len(dims) : 2 * len(dims)]
    load_sem, z_send, z_recv, p_send, p_recv = rest[2 * len(dims) :]
    n_block, _, rows, width = held.shape
    points = part.shape[0]
    snap = n_block * width
    row, col, z = (lax.axis_index(a) for a in ("row", "col", "grid"))
    place = {"core": col % 2, "y": col // 2, "row": row}

    def peer(kind, n, p):
        other = lax.rem(place[kind] + p, n)
        if kind == "row":
            return (other, col, z)
        if kind == "core":
            return (row, (col // 2) * 2 + other, z)
        return (row, other * 2 + col % 2, z)

    peers = [peer(kind, n, p) for n, kind in dims for p in range(1, n)]
    up, down = (row, col, z + 1), (row, col, z - 1)
    loads = [
        pltpu.make_async_copy(
            snaps_ref.at[:, pl.ds(k * width, width)], held.at[k, z], load_sem.at[k]
        )
        for k in range(n_block)
    ]
    for load in loads:
        load.start()
    barrier = pltpu.get_barrier_semaphore()
    for device in peers:
        pl.semaphore_signal(barrier, inc=1, device_id=device, device_id_type=MESH)

    @pl.when(z + 1 < n_grid)
    def _():
        pl.semaphore_signal(barrier, inc=1, device_id=up, device_id_type=MESH)

    @pl.when(z > 0)
    def _():
        pl.semaphore_signal(barrier, inc=1, device_id=down, device_id_type=MESH)

    beside = jnp.minimum(z, 1) + jnp.minimum(n_grid - 1 - z, 1)
    pl.semaphore_wait(barrier, len(peers) + beside)

    def hop(k, s, direction, origin):
        return pltpu.make_async_remote_copy(
            src_ref=held.at[k, origin],
            dst_ref=held.at[k, origin],
            send_sem=z_send.at[direction, k, s],
            recv_sem=z_recv.at[direction, k, s],
            device_id=up if direction == 0 else down,
            device_id_type=MESH,
        )

    def can_send(s, direction):
        if direction == 0:
            return jnp.logical_and(z + 1 < n_grid, z - s >= 0), z - s
        return jnp.logical_and(z > 0, z + s < n_grid), z + s

    def can_receive(s, direction):
        if direction == 0:
            return z - s - 1 >= 0, z - s - 1
        return z + s + 1 < n_grid, z + s + 1

    def send(k, s):
        for direction in (0, 1):
            ok, origin = can_send(s, direction)

            @pl.when(ok)
            def _():
                hop(k, s, direction, origin).start()

    def receive(k, s):
        for direction in (0, 1):
            ok, origin = can_receive(s, direction)

            @pl.when(ok)
            def _():
                hop(k, s, direction, origin).wait_recv()

    def drain(k, s):
        for direction in (0, 1):
            ok, origin = can_send(s, direction)

            @pl.when(ok)
            def _():
                hop(k, s, direction, origin).wait_send()

    def reduce_steps(source, target):
        lanes = pl.ds(0, source.shape[1])
        offsets, sems, at, count = [], [], 0, 0
        length = points
        for n, kind in dims:
            length //= n
            offsets.append((at, length))
            at = at + place[kind] * length
            sems.append(count)
            count += n - 1

        def aligned(index):
            return pl.multiple_of(index, 8)

        def scatter(a):
            n, kind = dims[a]
            size = offsets[a][1]
            cur = source if a == 0 else sums[a - 1].at[:, lanes]
            copies = []
            for p in range(1, n):
                other = lax.rem(place[kind] + p, n)
                copy = pltpu.make_async_remote_copy(
                    src_ref=cur.at[pl.ds(aligned(other * size), size), :],
                    dst_ref=landed[a].at[p - 1, :, lanes],
                    send_sem=p_send.at[0, sems[a] + p - 1],
                    recv_sem=p_recv.at[0, sems[a] + p - 1],
                    device_id=peer(kind, n, p),
                    device_id_type=MESH,
                )
                copy.start()
                copies.append(copy)
            for copy in copies:
                copy.wait()
            total = cur[pl.ds(aligned(place[kind] * size), size), :]
            for p in range(1, n):
                total = total + landed[a][p - 1, :, lanes]
            if a + 1 < len(dims):
                sums[a][:, lanes] = total
            else:
                target[pl.ds(aligned(at), size), :] = total

        def gather(a):
            n, kind = dims[a]
            base, size = offsets[a]
            mine = pl.ds(aligned(base + place[kind] * size), size)
            copies = []
            for p in range(1, n):
                copy = pltpu.make_async_remote_copy(
                    src_ref=target.at[mine, :],
                    dst_ref=target.at[mine, :],
                    send_sem=p_send.at[1, sems[a] + p - 1],
                    recv_sem=p_recv.at[1, sems[a] + p - 1],
                    device_id=peer(kind, n, p),
                    device_id_type=MESH,
                )
                copy.start()
                copies.append(copy)
            for copy in copies:
                copy.wait()

        steps = [functools.partial(scatter, a) for a in range(len(dims))]
        return steps + [functools.partial(gather, a) for a in reversed(range(len(dims)))]

    def steer():
        part_norm[...] = jnp.zeros_like(part_norm)
        tile = 16
        tiles = points // tile

        def body(i, carry):
            g, first = i // tiles, pl.multiple_of((i % tiles) * tile, tile)
            pos = pos_ref[g]
            point = start_ref[0] + stride * (
                first + lax.broadcasted_iota(jnp.int32, (tile, 1), 0)
            )
            phase = (point * pos - ((pos & 127) << 15)) << 10
            turns = phase.astype(F32) * F32(2.0**-32)
            value = sine(0.25 - jnp.abs(turns))
            hi, lo = split(value)
            steer_hi[g, pl.ds(first, tile), :] = hi
            steer_lo[g, pl.ds(first, tile), :] = lo
            square = jnp.sum(value * value, axis=1, keepdims=True)
            part_norm[pl.ds(first, tile), :] += jnp.broadcast_to(square, (tile, 128))
            return carry

        lax.fori_loop(0, n_grid * tiles, body, 0)

    def project(k):
        part[...] = jnp.zeros_like(part)

        def body(g, carry):
            block = held[k, g]
            part[...] += jnp.dot(steer_hi[g], block, preferred_element_type=F32) + jnp.dot(
                steer_lo[g], block, preferred_element_type=F32
            )
            return carry

        lax.fori_loop(0, n_grid, body, 0)

    def apply(k):
        value = full[k]
        square = jnp.sum(value * value, axis=1, keepdims=True)
        square = jnp.broadcast_to(square, (points, 128))
        forms_ref[...] = square if k == 0 else forms_ref[...] + square
        hi, lo = split(value / snap)
        proj_hi[...] = hi
        proj_lo[...] = lo
        dims_nt = (((1,), (1,)), ((), ()))

        def body(g, carry):
            block = held[k, g]
            added = lax.dot_general(block, proj_hi[...], dims_nt, preferred_element_type=F32)
            added += lax.dot_general(block, proj_lo[...], dims_nt, preferred_element_type=F32)
            spot = pl.ds(pl.multiple_of(g * rows, rows), rows)
            out_ref[spot, :] = added if k == 0 else out_ref[spot, :] + added
            return carry

        lax.fori_loop(0, n_grid, body, 0)

    loads[0].wait()
    send(0, 0)
    for load in loads[1:]:
        load.wait()
    steer()
    last = n_grid - 2
    queue = reduce_steps(part_norm, norms_ref)
    for k in range(n_block):
        for s in range(n_grid - 1):
            if k > 0 and s == 0:
                project(k - 1)
                queue = reduce_steps(part, full.at[k - 1])
            share = -(-len(queue) // (n_grid - 1 - s))
            todo, queue = queue[:share], queue[share:]
            for step in todo[:1]:
                step()
            receive(k, s)
            if s < last:
                send(k, s + 1)
            if s + 1 == last and k + 1 < n_block:
                send(k + 1, 0)
            for step in todo[1:]:
                step()
            if k > 1 and s == 0:
                apply(k - 2)
    project(n_block - 1)
    if n_block > 1:
        apply(n_block - 2)
    for step in reduce_steps(part, full.at[n_block - 1]):
        step()
    apply(n_block - 1)
    for k in range(n_block):
        for s in range(n_grid - 1):
            drain(k, s)


def on_device(snapshots, jitter_code, slab_start, gamma, noise_var):
    n_row, n_col, n_grid = (lax.axis_size(a) for a in ("row", "col", "grid"))
    rows, snap = snapshots.shape
    group_rows = rows * n_grid
    points = gamma.shape[0]
    base = (lax.axis_index("row") * n_col + lax.axis_index("col")) * group_rows
    sensors = base + jnp.arange(group_rows, dtype=jnp.int32)
    pos = 64 * sensors + lax.dynamic_slice(jitter_code, (base,), (group_rows,)) + 32
    width = min(WIDTH, snap)
    n_block = snap // width
    dims = [n for n in (2, n_col // 2, n_row) if n > 1]
    landed, sums, length = [], [], points
    for n in dims:
        length //= n
        landed.append(pltpu.VMEM((n - 1, length, width), F32))
        sums.append(pltpu.VMEM((length, width), F32))
    n_peers = sum(n - 1 for n in dims)
    vmem = pl.BlockSpec(memory_space=pltpu.VMEM)
    steered, forms, norms = pl.pallas_call(
        functools.partial(kernel, (n_row, n_col, n_grid, GRID // points)),
        out_shape=(
            jax.ShapeDtypeStruct((group_rows, points), F32),
            jax.ShapeDtypeStruct((points, 128), F32),
            jax.ShapeDtypeStruct((points, 128), F32),
        ),
        in_specs=[
            pl.BlockSpec(memory_space=pltpu.SMEM),
            vmem,
            pl.BlockSpec(memory_space=pl.ANY),
        ],
        out_specs=(vmem, vmem, vmem),
        scratch_shapes=[
            pltpu.VMEM((n_block, n_grid, rows, width), BF16),
            pltpu.VMEM((n_grid, points, rows), BF16),
            pltpu.VMEM((n_grid, points, rows), BF16),
            pltpu.VMEM((points, width), F32),
            pltpu.VMEM((points, 128), F32),
            pltpu.VMEM((n_block, points, width), F32),
            pltpu.VMEM((points, width), BF16),
            pltpu.VMEM((points, width), BF16),
            *landed,
            *sums,
            pltpu.SemaphoreType.DMA((n_block,)),
            pltpu.SemaphoreType.DMA((2, n_block, n_grid - 1)),
            pltpu.SemaphoreType.DMA((2, n_block, n_grid - 1)),
            pltpu.SemaphoreType.DMA((2, n_peers)),
            pltpu.SemaphoreType.DMA((2, n_peers)),
        ],
        compiler_params=pltpu.CompilerParams(
            collective_id=0, has_side_effects=True, vmem_limit_bytes=56 << 20
        ),
    )(slab_start, pos.reshape(n_grid, 1, rows), snapshots)
    forms = forms[:, 0] / snap
    gamma_new = gamma * forms / (norms[:, 0] * (gamma + noise_var[0]))
    return (steered, gamma_new)


def solution(mesh):
    in_specs = (P(("row", "col", "grid"), None), P(), P("grid"), P("grid"), P())
    out_specs = (P(("row", "col"), "grid"), P("grid"))
    return jax.shard_map(
        on_device, mesh=mesh, in_specs=in_specs, out_specs=out_specs, check_vma=False
    )
```

time: 206 us -> 139 us (0.67)
  Pallas kernels: 0 us -> 127 us
  waiting for transfers between devices: 98.8 us -> 0 us
  matrix products: 39.4 us -> 0 us
  other arithmetic: 21.5 us -> 3.82 us
  blocking collectives: 13.7 us -> 0 us
  between operations: 15.4 us -> 1.96 us
  local copies, waits for them, and re-layouts: 17.3 us -> 4.64 us
    pallas_call x0 -> x1, Pallas kernels: none -> 127 us  [on_device(): pl.pallas_call(functools.partial(kernel, (n_row, n_col, n_grid, GRID // p...]
    all_gather x1 -> x0, waiting for transfers between devices: 71.9 us -> none  [on_device(): lax.all_gather(snapshots, 'grid', axis=0, tiled=True).astype(jnp.float32)]
    dot_general x2 -> x0, matrix products: 39.4 us -> none  [the longest x1 28.9 us: on_device(): jnp.dot(own_snaps.T, own_steer, precision=lax.Precision.HIGHEST)]
    psum x1 -> x0, waiting for transfers between devices: 26.2 us -> none  [on_device(): lax.psum((partial_value, jnp.sum(own_steer * own_steer, axis=0)), ('row',...]
    reduce_sum x2 -> x0, other arithmetic: 20.8 us -> none  [the longest x1 20.6 us: on_device(): jnp.sum(own_steer * own_steer, axis=0)]
    psum x1 -> x0, blocking collectives: 13.7 us -> none  [on_device(): lax.psum((partial_value, jnp.sum(own_steer * own_steer, axis=0)), ('row',...]
    gather x1 -> x0, local copies, waits for them, and re-layouts: 11.8 us -> none  [on_device(): own_steer = steer(own_sensors, jnp.take(jitter_code, own_sensors), points)]
    unnamed x7 -> x1, local copies, waits for them, and re-layouts: 5.51 us -> 4.64 us
  transfers between devices with their start and end apart: 2 -> 0, of which waited for: 2 -> 0; matrix products, arithmetic and copies ran while one was open for 16% -> 0% of each run, Pallas kernels for 0% -> 0%
where the time goes in v2:
time: 139 us; the launch traced here: 138 us
  Pallas kernels  127 us (91%)
  local copies, waits for them, and re-layouts  4.64 us (3%)
  other arithmetic  3.82 us (3%)
  between operations  1.96 us (1%)
    pallas_call x1, Pallas kernels, on_device(): pl.pallas_call(functools.partial(kernel, (n_row, n_col, n_grid, GRID // p...  127 us
    unnamed x1, local copies, waits for them, and re-layouts  4.64 us

profile of v2, /device:TPU:0, one launch (start us, length us, event | category | flops | bytes accessed | tf_op | source)
XLA Modules:
  0.0 137.5 jit_solution(8434596981900453336)
XLA Ops:
  0.6 1.3 add_add_fusion
  2.6 127.1 %shard_map.68 = (f32[2048,512]{1,0:T(8,128)}, f32[512,128]{1,0:T(8,128)}, f32[512,128]{1,0:T(8,128)}) custom-call(s32[1]{0:T(128)S(6)} %copy.8.start_ref, s32[4,1,512]{2,1,0:T(1,128)} %bitcast.3, bf16[512,1024]{1,0:T(8,128)(2,1)} %snaps_ref.1), custom_call_target="tpu_custom_call" | custom-call | tf_op jit(solution)/shard_map/pallas_call | solution.py:295
  129.7 1.2 slice_reduce_fusion
  131.6 1.3 multiply_divide_fusion
  132.9 4.6 %copy.10 = f32[2048,512]{1,0:T(8,128)} copy(f32[2048,512]{1,0:T(8,128)} %get-tuple-element.12) | data formatting | bytes 8388608

commit v3 on v2

--- a/solution.py
+++ b/solution.py
@@ -38,7 +38,7 @@
     landed, sums = rest[: len(dims)], rest[len(dims) : 2 * len(dims)]
     load_sem, z_send, z_recv, p_send, p_recv = rest[2 * len(dims) :]
     n_block, _, rows, width = held.shape
-    points = part.shape[0]
+    points = part.shape[1]
     snap = n_block * width
     row, col, z = (lax.axis_index(a) for a in ("row", "col", "grid"))
     place = {"core": col % 2, "y": col // 2, "row": row}
@@ -139,6 +139,7 @@
             size = offsets[a][1]
             cur = source if a == 0 else sums[a - 1].at[:, lanes]
             copies = []
+            yield
             for p in range(1, n):
                 other = lax.rem(place[kind] + p, n)
                 copy = pltpu.make_async_remote_copy(
@@ -151,6 +152,7 @@
                 )
                 copy.start()
                 copies.append(copy)
+            yield
             for copy in copies:
                 copy.wait()
             total = cur[pl.ds(aligned(place[kind] * size), size), :]
@@ -160,12 +162,14 @@
                 sums[a][:, lanes] = total
             else:
                 target[pl.ds(aligned(at), size), :] = total
+            yield
 
         def gather(a):
             n, kind = dims[a]
             base, size = offsets[a]
             mine = pl.ds(aligned(base + place[kind] * size), size)
             copies = []
+            yield
             for p in range(1, n):
                 copy = pltpu.make_async_remote_copy(
                     src_ref=target.at[mine, :],
@@ -177,11 +181,16 @@
                 )
                 copy.start()
                 copies.append(copy)
+            yield
             for copy in copies:
                 copy.wait()
-
-        steps = [functools.partial(scatter, a) for a in range(len(dims))]
-        return steps + [functools.partial(gather, a) for a in reversed(range(len(dims)))]
+            yield
+
+        steps = [scatter(a) for a in range(len(dims))]
+        steps += [gather(a) for a in reversed(range(len(dims)))]
+        for step in steps:
+            next(step)
+        return steps
 
     def steer():
         part_norm[...] = jnp.zeros_like(part_norm)
@@ -206,19 +215,24 @@
 
         lax.fori_loop(0, n_grid * tiles, body, 0)
 
-    def project(k):
-        part[...] = jnp.zeros_like(part)
-
-        def body(g, carry):
-            block = held[k, g]
-            part[...] += jnp.dot(steer_hi[g], block, preferred_element_type=F32) + jnp.dot(
-                steer_lo[g], block, preferred_element_type=F32
-            )
-            return carry
-
-        lax.fori_loop(0, n_grid, body, 0)
-
-    def apply(k):
+    def project(k, origin, fresh=False):
+        block = held[k, origin]
+        value = jnp.dot(steer_hi[origin], block, preferred_element_type=F32)
+        value += jnp.dot(steer_lo[origin], block, preferred_element_type=F32)
+        if fresh:
+            part[k % 2] = value
+        else:
+            part[k % 2] += value
+
+    def project_arrived(k, s):
+        for direction in (0, 1):
+            ok, origin = can_receive(s, direction)
+
+            @pl.when(ok)
+            def _():
+                project(k, origin)
+
+    def prepare(k):
         value = full[k]
         square = jnp.sum(value * value, axis=1, keepdims=True)
         square = jnp.broadcast_to(square, (points, 128))
@@ -226,6 +240,8 @@
         hi, lo = split(value / snap)
         proj_hi[...] = hi
         proj_lo[...] = lo
+
+    def apply(k, first, count):
         dims_nt = (((1,), (1,)), ((), ()))
 
         def body(g, carry):
@@ -236,39 +252,57 @@
             out_ref[spot, :] = added if k == 0 else out_ref[spot, :] + added
             return carry
 
-        lax.fori_loop(0, n_grid, body, 0)
+        lax.fori_loop(first, first + count, body, 0)
+
+    def applied(k, s, rounds):
+        if k < 0:
+            return
+        if s == 0:
+            prepare(k)
+        first, end = n_grid * s // rounds, n_grid * (s + 1) // rounds
+        if end > first:
+            apply(k, first, end - first)
 
     loads[0].wait()
     send(0, 0)
-    for load in loads[1:]:
+    if n_block > 1:
+        loads[1].wait()
+        send(1, 0)
+    for load in loads[2:]:
         load.wait()
     steer()
-    last = n_grid - 2
+    rounds = n_grid - 1
     queue = reduce_steps(part_norm, norms_ref)
     for k in range(n_block):
-        for s in range(n_grid - 1):
-            if k > 0 and s == 0:
-                project(k - 1)
-                queue = reduce_steps(part, full.at[k - 1])
-            share = -(-len(queue) // (n_grid - 1 - s))
+        for s in range(rounds):
+            share = -(-len(queue) // (rounds - s))
             todo, queue = queue[:share], queue[share:]
             for step in todo[:1]:
-                step()
+                next(step)
+            if s == 0:
+                project(k, z, fresh=True)
             receive(k, s)
-            if s < last:
+            if s + 1 < rounds:
                 send(k, s + 1)
-            if s + 1 == last and k + 1 < n_block:
-                send(k + 1, 0)
-            for step in todo[1:]:
-                step()
-            if k > 1 and s == 0:
-                apply(k - 2)
-    project(n_block - 1)
-    if n_block > 1:
-        apply(n_block - 2)
-    for step in reduce_steps(part, full.at[n_block - 1]):
-        step()
-    apply(n_block - 1)
+            if s + 2 == rounds and k + 2 < n_block:
+                send(k + 2, 0)
+            for step in todo[:1]:
+                next(step)
+            for step in todo[1:2]:
+                next(step)
+            project_arrived(k, s)
+            applied(k - 2, s, rounds)
+            for step in todo[1:2]:
+                next(step)
+            for step in todo[2:]:
+                next(step)
+                next(step)
+        queue = reduce_steps(part.at[k % 2], full.at[k])
+    for i, step in enumerate(queue):
+        next(step)
+        applied(n_block - 2, i, len(queue))
+        next(step)
+    applied(n_block - 1, 0, 1)
     for k in range(n_block):
         for s in range(n_grid - 1):
             drain(k, s)
@@ -309,7 +343,7 @@
             pltpu.VMEM((n_block, n_grid, rows, width), BF16),
             pltpu.VMEM((n_grid, points, rows), BF16),
             pltpu.VMEM((n_grid, points, rows), BF16),
-            pltpu.VMEM((points, width), F32),
+            pltpu.VMEM((2, points, width), F32),
             pltpu.VMEM((points, 128), F32),
             pltpu.VMEM((n_block, points, width), F32),
             pltpu.VMEM((points, width), BF16),

time: 139 us -> 124 us (0.89)
  Pallas kernels: 127 us -> 113 us
    pallas_call x1, Pallas kernels: 127 us -> 113 us  [on_device(): pl.pallas_call(functools.partial(kernel, (n_row, n_col, n_grid, GRID // p...]
where the time goes in v3:
time: 124 us; the launch traced here: 123 us
  Pallas kernels  113 us (91%)
  local copies, waits for them, and re-layouts  4.64 us (4%)
  other arithmetic  3.82 us (3%)
  between operations  1.96 us (2%)
    pallas_call x1, Pallas kernels, on_device(): pl.pallas_call(functools.partial(kernel, (n_row, n_col, n_grid, GRID // p...  113 us
    unnamed x1, local copies, waits for them, and re-layouts  4.64 us

profile of v3, /device:TPU:0, one launch (start us, length us, event | category | flops | bytes accessed | tf_op | source)
XLA Modules:
  0.0 123.4 jit_solution(17127785648954888558)
XLA Ops:
  0.6 1.3 %add_add_fusion = s32[2048]{0:T(1024)} fusion(s32[16384]{0:T(1024)} %param.6, s32[]{:T(128)S(6)} %select_n.3, s32[]{:T(128)S(6)} %mul.19), kind=kLoop, calls=%fused_computation.2 | loop fusion | flops 8192 | bytes 16392 | tf_op jit(solution)/shard_map/add | solution.py:318
  2.6 112.9 %shard_map.68 = (f32[2048,512]{1,0:T(8,128)}, f32[512,128]{1,0:T(8,128)}, f32[512,128]{1,0:T(8,128)}) custom-call(s32[1]{0:T(128)S(6)} %copy.8.start_ref, s32[4,1,512]{2,1,0:T(1,128)} %bitcast.3, bf16[512,1024]{1,0:T(8,128)(2,1)} %snaps_ref.1), custom_call_target="tpu_custom_call" | custom-call | tf_op jit(solution)/shard_map/pallas_call | solution.py:329
  115.5 1.2 %slice_reduce_fusion = (f32[512]{0:T(512)S(1)}, f32[512]{0:T(512)S(1)}) fusion(f32[512,128]{1,0:T(8,128)} %get-tuple-element.7, f32[512,128]{1,0:T(8,128)} %get-tuple-element.6), kind=kLoop, calls=%fused_computation | loop fusion | flops 512 | bytes 8192 | tf_op jit(solution)/shard_map/slice | solution.py:364
  117.4 1.3 %multiply_divide_fusion = f32[512]{0:T(512)} fusion(f32[512]{0:T(512)S(1)} %get-tuple-element.8, f32[512]{0:T(512)} %param.8, f32[512]{0:T(512)S(1)} %get-tuple-element.9, f32[]{:T(128)} %bitcast.2), kind=kLoop, calls=%fused_computation.3 | loop fusion | flops 2048 | bytes 8196 | tf_op jit(solution)/shard_map/div | solution.py:364
  118.7 4.6 %copy.10 = f32[2048,512]{1,0:T(8,128)} copy(f32[2048,512]{1,0:T(8,128)} %get-tuple-element.12) | data formatting | bytes 8388608

commit v4 on v3

--- a/solution.py
+++ b/solution.py
@@ -120,7 +120,7 @@
             def _():
                 hop(k, s, direction, origin).wait_send()
 
-    def reduce_steps(source, target):
+    def reduce_steps(source, target, turn):
         lanes = pl.ds(0, source.shape[1])
         offsets, sems, at, count = [], [], 0, 0
         length = points
@@ -144,9 +144,9 @@
                 other = lax.rem(place[kind] + p, n)
                 copy = pltpu.make_async_remote_copy(
                     src_ref=cur.at[pl.ds(aligned(other * size), size), :],
-                    dst_ref=landed[a].at[p - 1, :, lanes],
-                    send_sem=p_send.at[0, sems[a] + p - 1],
-                    recv_sem=p_recv.at[0, sems[a] + p - 1],
+                    dst_ref=landed[a].at[turn, p - 1, :, lanes],
+                    send_sem=p_send.at[2 * turn, sems[a] + p - 1],
+                    recv_sem=p_recv.at[2 * turn, sems[a] + p - 1],
                     device_id=peer(kind, n, p),
                     device_id_type=MESH,
                 )
@@ -157,7 +157,7 @@
                 copy.wait()
             total = cur[pl.ds(aligned(place[kind] * size), size), :]
             for p in range(1, n):
-                total = total + landed[a][p - 1, :, lanes]
+                total = total + landed[a][turn, p - 1, :, lanes]
             if a + 1 < len(dims):
                 sums[a][:, lanes] = total
             else:
@@ -174,8 +174,8 @@
                 copy = pltpu.make_async_remote_copy(
                     src_ref=target.at[mine, :],
                     dst_ref=target.at[mine, :],
-                    send_sem=p_send.at[1, sems[a] + p - 1],
-                    recv_sem=p_recv.at[1, sems[a] + p - 1],
+                    send_sem=p_send.at[2 * turn + 1, sems[a] + p - 1],
+                    recv_sem=p_recv.at[2 * turn + 1, sems[a] + p - 1],
                     device_id=peer(kind, n, p),
                     device_id_type=MESH,
                 )
@@ -186,11 +186,11 @@
                 copy.wait()
             yield
 
-        steps = [scatter(a) for a in range(len(dims))]
-        steps += [gather(a) for a in reversed(range(len(dims)))]
-        for step in steps:
+        scatters = [scatter(a) for a in range(len(dims))]
+        gathers = [gather(a) for a in reversed(range(len(dims)))]
+        for step in scatters + gathers:
             next(step)
-        return steps
+        return scatters, gathers
 
     def steer():
         part_norm[...] = jnp.zeros_like(part_norm)
@@ -272,13 +272,22 @@
         load.wait()
     steer()
     rounds = n_grid - 1
-    queue = reduce_steps(part_norm, norms_ref)
+    def advance(steps):
+        for step in steps:
+            next(step)
+
+    def extra(*lists):
+        for steps in lists:
+            for step in steps[rounds:]:
+                next(step)
+                next(step)
+
+    scatters, gathers = reduce_steps(part_norm, norms_ref, 1)
+    waiting = []
     for k in range(n_block):
         for s in range(rounds):
-            share = -(-len(queue) // (rounds - s))
-            todo, queue = queue[:share], queue[share:]
-            for step in todo[:1]:
-                next(step)
+            slot = scatters[s : s + 1] + waiting[s : s + 1]
+            advance(slot)
             if s == 0:
                 project(k, z, fresh=True)
             receive(k, s)
@@ -286,22 +295,22 @@
                 send(k, s + 1)
             if s + 2 == rounds and k + 2 < n_block:
                 send(k + 2, 0)
-            for step in todo[:1]:
-                next(step)
-            for step in todo[1:2]:
-                next(step)
             project_arrived(k, s)
-            applied(k - 2, s, rounds)
-            for step in todo[1:2]:
-                next(step)
-            for step in todo[2:]:
-                next(step)
-                next(step)
-        queue = reduce_steps(part.at[k % 2], full.at[k])
-    for i, step in enumerate(queue):
-        next(step)
-        applied(n_block - 2, i, len(queue))
-        next(step)
+            applied(k - 3, s, rounds)
+            advance(slot)
+        extra(scatters, waiting)
+        waiting = gathers
+        scatters, gathers = reduce_steps(part.at[k % 2], full.at[k], k % 2)
+    for steps, others, block in (
+        (scatters, waiting, n_block - 3),
+        (gathers, [], n_block - 2),
+    ):
+        for s in range(rounds):
+            slot = steps[s : s + 1] + others[s : s + 1]
+            advance(slot)
+            applied(block, s, rounds)
+            advance(slot)
+        extra(steps, others)
     applied(n_block - 1, 0, 1)
     for k in range(n_block):
         for s in range(n_grid - 1):
@@ -322,7 +331,7 @@
     landed, sums, length = [], [], points
     for n in dims:
         length //= n
-        landed.append(pltpu.VMEM((n - 1, length, width), F32))
+        landed.append(pltpu.VMEM((2, n - 1, length, width), F32))
         sums.append(pltpu.VMEM((length, width), F32))
     n_peers = sum(n - 1 for n in dims)
     vmem = pl.BlockSpec(memory_space=pltpu.VMEM)
@@ -353,8 +362,8 @@
             pltpu.SemaphoreType.DMA((n_block,)),
             pltpu.SemaphoreType.DMA((2, n_block, n_grid - 1)),
             pltpu.SemaphoreType.DMA((2, n_block, n_grid - 1)),
-            pltpu.SemaphoreType.DMA((2, n_peers)),
-            pltpu.SemaphoreType.DMA((2, n_peers)),
+            pltpu.SemaphoreType.DMA((4, n_peers)),
+            pltpu.SemaphoreType.DMA((4, n_peers)),
         ],
         compiler_params=pltpu.CompilerParams(
             collective_id=0, has_side_effects=True, vmem_limit_bytes=56 << 20

time: 124 us -> 118 us (0.952)
  Pallas kernels: 113 us -> 107 us
    pallas_call x1, Pallas kernels: 113 us -> 107 us  [on_device(): pl.pallas_call(functools.partial(kernel, (n_row, n_col, n_grid, GRID // p...]
where the time goes in v4:
time: 118 us
  Pallas kernels  107 us (91%)
  local copies, waits for them, and re-layouts  4.64 us (4%)
  other arithmetic  3.82 us (3%)
  between operations  1.96 us (2%)
    pallas_call x1, Pallas kernels, on_device(): pl.pallas_call(functools.partial(kernel, (n_row, n_col, n_grid, GRID // p...  107 us
    unnamed x1, local copies, waits for them, and re-layouts  4.64 us

profile of v4, /device:TPU:0, one launch (start us, length us, event | category | flops | bytes accessed | tf_op | source)
XLA Modules:
  0.0 117.9 jit_solution(1566628744369546405)
XLA Ops:
  0.6 1.3 %add_add_fusion = s32[2048]{0:T(1024)} fusion(s32[16384]{0:T(1024)} %param.6, s32[]{:T(128)S(6)} %select_n.3, s32[]{:T(128)S(6)} %mul.19), kind=kLoop, calls=%fused_computation.2 | loop fusion | flops 8192 | bytes 16392 | tf_op jit(solution)/shard_map/add | solution.py:327
  2.6 107.5 %shard_map.68 = (f32[2048,512]{1,0:T(8,128)}, f32[512,128]{1,0:T(8,128)}, f32[512,128]{1,0:T(8,128)}) custom-call(s32[1]{0:T(128)S(6)} %copy.8.start_ref, s32[4,1,512]{2,1,0:T(1,128)} %bitcast.3, bf16[512,1024]{1,0:T(8,128)(2,1)} %snaps_ref.1), custom_call_target="tpu_custom_call" | custom-call | tf_op jit(solution)/shard_map/pallas_call | solution.py:338
  110.1 1.2 %slice_reduce_fusion = (f32[512]{0:T(512)S(1)}, f32[512]{0:T(512)S(1)}) fusion(f32[512,128]{1,0:T(8,128)} %get-tuple-element.7, f32[512,128]{1,0:T(8,128)} %get-tuple-element.6), kind=kLoop, calls=%fused_computation | loop fusion | flops 512 | bytes 8192 | tf_op jit(solution)/shard_map/slice | solution.py:373
  112.0 1.3 %multiply_divide_fusion = f32[512]{0:T(512)} fusion(f32[512]{0:T(512)S(1)} %get-tuple-element.8, f32[512]{0:T(512)} %param.8, f32[512]{0:T(512)S(1)} %get-tuple-element.9, f32[]{:T(128)} %bitcast.2), kind=kLoop, calls=%fused_computation.3 | loop fusion | flops 2048 | bytes 8196 | tf_op jit(solution)/shard_map/div | solution.py:373
  113.3 4.6 %copy.10 = f32[2048,512]{1,0:T(8,128)} copy(f32[2048,512]{1,0:T(8,128)} %get-tuple-element.12) | data formatting | bytes 8388608

commit v5 on v4

--- a/solution.py
+++ b/solution.py
@@ -30,8 +30,8 @@
 
 
 def kernel(
-    sizes, start_ref, pos_ref, snaps_ref, out_ref, forms_ref, norms_ref,
-    held, steer_hi, steer_lo, part, part_norm, full, proj_hi, proj_lo, *rest,
+    sizes, start_ref, pos_ref, snaps_ref, out_ref, forms_ref, norms_ref, last_ref, proj_hi, proj_lo,
+    held, steer_hi, steer_lo, part, part_norm, full, *rest,
 ):
     n_row, n_col, n_grid, stride = sizes
     dims = [d for d in ((2, "core"), (n_col // 2, "y"), (n_row, "row")) if d[0] > 1]
@@ -301,6 +301,7 @@
         extra(scatters, waiting)
         waiting = gathers
         scatters, gathers = reduce_steps(part.at[k % 2], full.at[k], k % 2)
+    last_ref[...] = held[n_block - 1]
     for steps, others, block in (
         (scatters, waiting, n_block - 3),
         (gathers, [], n_block - 2),
@@ -311,10 +312,18 @@
             applied(block, s, rounds)
             advance(slot)
         extra(steps, others)
-    applied(n_block - 1, 0, 1)
+    prepare(n_block - 1)
     for k in range(n_block):
         for s in range(n_grid - 1):
             drain(k, s)
+
+
+def finish(partly_ref, held_ref, hi_ref, lo_ref, out_ref):
+    dims_nt = (((1,), (1,)), ((), ()))
+    block = held_ref[0]
+    added = lax.dot_general(block, hi_ref[...], dims_nt, preferred_element_type=F32)
+    added += lax.dot_general(block, lo_ref[...], dims_nt, preferred_element_type=F32)
+    out_ref[...] = partly_ref[...] + added
 
 
 def on_device(snapshots, jitter_code, slab_start, gamma, noise_var):
@@ -335,19 +344,22 @@
         sums.append(pltpu.VMEM((length, width), F32))
     n_peers = sum(n - 1 for n in dims)
     vmem = pl.BlockSpec(memory_space=pltpu.VMEM)
-    steered, forms, norms = pl.pallas_call(
+    partly, forms, norms, held, proj_hi, proj_lo = pl.pallas_call(
         functools.partial(kernel, (n_row, n_col, n_grid, GRID // points)),
         out_shape=(
             jax.ShapeDtypeStruct((group_rows, points), F32),
             jax.ShapeDtypeStruct((points, 128), F32),
             jax.ShapeDtypeStruct((points, 128), F32),
+            jax.ShapeDtypeStruct((n_grid, rows, width), BF16),
+            jax.ShapeDtypeStruct((points, width), BF16),
+            jax.ShapeDtypeStruct((points, width), BF16),
         ),
         in_specs=[
             pl.BlockSpec(memory_space=pltpu.SMEM),
             vmem,
             pl.BlockSpec(memory_space=pl.ANY),
         ],
-        out_specs=(vmem, vmem, vmem),
+        out_specs=(vmem,) * 6,
         scratch_shapes=[
             pltpu.VMEM((n_block, n_grid, rows, width), BF16),
             pltpu.VMEM((n_grid, points, rows), BF16),
@@ -355,8 +367,6 @@
             pltpu.VMEM((2, points, width), F32),
             pltpu.VMEM((points, 128), F32),
             pltpu.VMEM((n_block, points, width), F32),
-            pltpu.VMEM((points, width), BF16),
-            pltpu.VMEM((points, width), BF16),
             *landed,
             *sums,
             pltpu.SemaphoreType.DMA((n_block,)),
@@ -369,6 +379,15 @@
             collective_id=0, has_side_effects=True, vmem_limit_bytes=56 << 20
         ),
     )(slab_start, pos.reshape(n_grid, 1, rows), snapshots)
+    whole = pl.BlockSpec((points, width), lambda i: (0, 0))
+    tile = pl.BlockSpec((rows, points), lambda i: (i, 0))
+    steered = pl.pallas_call(
+        finish,
+        grid=(n_grid,),
+        out_shape=jax.ShapeDtypeStruct((group_rows, points), F32),
+        in_specs=[tile, pl.BlockSpec((1, rows, width), lambda i: (i, 0, 0)), whole, whole],
+        out_specs=tile,
+    )(partly, held, proj_hi, proj_lo)
     forms = forms[:, 0] / snap
     gamma_new = gamma * forms / (norms[:, 0] * (gamma + noise_var[0]))
     return (steered, gamma_new)

time: 118 us -> 118 us (level)
  Pallas kernels: 107 us -> 112 us
  local copies, waits for them, and re-layouts: 4.64 us -> 0 us
    pallas_call x0 -> x1, Pallas kernels: none -> 5.88 us  [on_device(): pl.pallas_call(finish, grid=(n_grid,), out_shape=jax.ShapeDtypeStruct((gr...]
    unnamed x1 -> x0, local copies, waits for them, and re-layouts: 4.64 us -> none
    pallas_call x1, Pallas kernels: 107 us -> 106 us  [on_device(): pl.pallas_call(functools.partial(kernel, (n_row, n_col, n_grid, GRID // p...]
where the time goes in v5:
time: 118 us
  Pallas kernels  112 us (95%)
  other arithmetic  3.82 us (3%)
  between operations  1.96 us (2%)
    pallas_call x1, Pallas kernels, on_device(): pl.pallas_call(functools.partial(kernel, (n_row, n_col, n_grid, GRID // p...  106 us
    pallas_call x1, Pallas kernels, on_device(): pl.pallas_call(finish, grid=(n_grid,), out_shape=jax.ShapeDtypeStruct((gr...  5.88 us

profile of v5, /device:TPU:0, one launch (start us, length us, event | category | flops | bytes accessed | tf_op | source)
XLA Modules:
  0.0 117.8 jit_solution(4373515182520937649)
XLA Ops:
  0.6 1.3 %add_add_fusion = s32[2048]{0:T(1024)} fusion(s32[16384]{0:T(1024)} %param.6, s32[]{:T(128)S(6)} %select_n.3, s32[]{:T(128)S(6)} %mul.19), kind=kLoop, calls=%fused_computation.2 | loop fusion | flops 8192 | bytes 16392 | tf_op jit(solution)/shard_map/add | solution.py:336
  2.6 106.2 %shard_map.68 = (f32[2048,512]{1,0:T(8,128)}, f32[512,128]{1,0:T(8,128)}, f32[512,128]{1,0:T(8,128)}, bf16[4,512,256]{2,1,0:T(8,128)(2,1)}, bf16[512,256]{1,0:T(8,128)(2,1)}, /*index=5*/bf16[512,256]{1,0:T(8,128)(2,1)}) custom-call(s32[1]{0:T(128)S(6)} %copy.7.start_ref, s32[4,1,512]{2,1,0:T(1,128)} %bitcast.3, bf16[512,1024]{1,0:T(8,128)(2,1)} %snaps_ref.1), custom_call_target="tpu_custom_call" | custom-call | tf_op jit(solution)/shard_map/pallas_call | solution.py:347
  108.8 1.2 %slice_reduce_fusion = (f32[512]{0:T(512)S(1)}, f32[512]{0:T(512)S(1)}) fusion(f32[512,128]{1,0:T(8,128)} %get-tuple-element.13, f32[512,128]{1,0:T(8,128)} %get-tuple-element.12), kind=kLoop, calls=%fused_computation | loop fusion | flops 512 | bytes 8192 | tf_op jit(solution)/shard_map/slice | solution.py:392
  110.7 1.3 %multiply_divide_fusion = f32[512]{0:T(512)} fusion(f32[512]{0:T(512)S(1)} %get-tuple-element.14, f32[512]{0:T(512)} %param.8, f32[512]{0:T(512)S(1)} %get-tuple-element.15, f32[]{:T(128)} %bitcast.2), kind=kLoop, calls=%fused_computation.3 | loop fusion | flops 2048 | bytes 8196 | tf_op jit(solution)/shard_map/div | solution.py:392
  112.0 5.9 %shard_map.69 = f32[2048,512]{1,0:T(8,128)} custom-call(f32[2048,512]{1,0:T(8,128)} %get-tuple-element.8.partly_ref, bf16[4,512,256]{2,1,0:T(8,128)(2,1)} %get-tuple-element.9.held_ref, bf16[512,256]{1,0:T(8,128)(2,1)} %get-tuple-element.10.hi_ref, bf16[512,256]{1,0:T(8,128)(2,1)} %get-tuple-element.11.lo_ref), custom_call_target="tpu_custom_call" | custom-call | tf_op jit(solution)/shard_map/pallas_call | solution.py:384

commit v6 on v5

--- a/solution.py
+++ b/solution.py
@@ -288,13 +288,13 @@
         for s in range(rounds):
             slot = scatters[s : s + 1] + waiting[s : s + 1]
             advance(slot)
-            if s == 0:
-                project(k, z, fresh=True)
             receive(k, s)
             if s + 1 < rounds:
                 send(k, s + 1)
             if s + 2 == rounds and k + 2 < n_block:
                 send(k + 2, 0)
+            if s == 0:
+                project(k, z, fresh=True)
             project_arrived(k, s)
             applied(k - 3, s, rounds)
             advance(slot)

time: 118 us -> 118 us (level)
  no operation moved by 1% of the time
where the time goes in v6:
time: 118 us; the launch traced here: 117 us
  Pallas kernels  112 us (95%)
  other arithmetic  3.82 us (3%)
  between operations  1.96 us (2%)
    pallas_call x1, Pallas kernels, on_device(): pl.pallas_call(functools.partial(kernel, (n_row, n_col, n_grid, GRID // p...  106 us
    pallas_call x1, Pallas kernels, on_device(): pl.pallas_call(finish, grid=(n_grid,), out_shape=jax.ShapeDtypeStruct((gr...  5.87 us

profile of v6, /device:TPU:0, one launch (start us, length us, event | category | flops | bytes accessed | tf_op | source)
XLA Modules:
  0.0 117.4 jit_solution(16501196158931082336)
XLA Ops:
  0.6 1.3 %add_add_fusion = s32[2048]{0:T(1024)} fusion(s32[16384]{0:T(1024)} %param.6, s32[]{:T(128)S(6)} %select_n.3, s32[]{:T(128)S(6)} %mul.19), kind=kLoop, calls=%fused_computation.2 | loop fusion | flops 8192 | bytes 16392 | tf_op jit(solution)/shard_map/add | solution.py:336
  2.6 105.7 %shard_map.68 = (f32[2048,512]{1,0:T(8,128)}, f32[512,128]{1,0:T(8,128)}, f32[512,128]{1,0:T(8,128)}, bf16[4,512,256]{2,1,0:T(8,128)(2,1)}, bf16[512,256]{1,0:T(8,128)(2,1)}, /*index=5*/bf16[512,256]{1,0:T(8,128)(2,1)}) custom-call(s32[1]{0:T(128)S(6)} %copy.7.start_ref, s32[4,1,512]{2,1,0:T(1,128)} %bitcast.3, bf16[512,1024]{1,0:T(8,128)(2,1)} %snaps_ref.1), custom_call_target="tpu_custom_call" | custom-call | tf_op jit(solution)/shard_map/pallas_call | solution.py:347
  108.3 1.2 %slice_reduce_fusion = (f32[512]{0:T(512)S(1)}, f32[512]{0:T(512)S(1)}) fusion(f32[512,128]{1,0:T(8,128)} %get-tuple-element.13, f32[512,128]{1,0:T(8,128)} %get-tuple-element.12), kind=kLoop, calls=%fused_computation | loop fusion | flops 512 | bytes 8192 | tf_op jit(solution)/shard_map/slice | solution.py:392
  110.2 1.3 %multiply_divide_fusion = f32[512]{0:T(512)} fusion(f32[512]{0:T(512)S(1)} %get-tuple-element.14, f32[512]{0:T(512)} %param.8, f32[512]{0:T(512)S(1)} %get-tuple-element.15, f32[]{:T(128)} %bitcast.2), kind=kLoop, calls=%fused_computation.3 | loop fusion | flops 2048 | bytes 8196 | tf_op jit(solution)/shard_map/div | solution.py:392
  111.5 5.9 %shard_map.69 = f32[2048,512]{1,0:T(8,128)} custom-call(f32[2048,512]{1,0:T(8,128)} %get-tuple-element.8.partly_ref, bf16[4,512,256]{2,1,0:T(8,128)(2,1)} %get-tuple-element.9.held_ref, bf16[512,256]{1,0:T(8,128)(2,1)} %get-tuple-element.10.hi_ref, bf16[512,256]{1,0:T(8,128)(2,1)} %get-tuple-element.11.lo_ref), custom_call_target="tpu_custom_call" | custom-call | tf_op jit(solution)/shard_map/pallas_call | solution.py:384
